TPU v7x, 256 devices: a whole 4x4x8 slice. The times are simulated.
256 devices in a mesh: batch: 8 (over z), col: 32 (over y, x, core).
Axes of the slice: x: 4, y: 4, z: 8, core: 2. Of those that a mesh axis runs over, the one named last changes fastest.
Arguments:
- views: bfloat16 [2, 1024, 4096], P(None, 'batch', 'col'), may hold values from -132 to 132
- norm_scale_gain: float32 [4096], P('col'), may hold values from 0.5 to 1.5
- norm_shift_bias: float32 [4096], P('col'), may hold values from -3 to 3
- weight: bfloat16 [4096, 8192], P(None, 'col'), may hold values from -0.09375 to 0.09375
Outputs:
- loss: float32 [], replicated
- grad_weight: float32 [4096, 8192], P('batch', 'col')
- grad_gain: float32 [4096], P('col')
- grad_bias: float32 [4096], P('col')
- views_gradient: float32 [2, 1024, 4096], P(None, 'batch', 'col')
All inputs are finite; a program needn't handle non-finite values.
Results may differ from a plain program's by a relative error of at most 0.0027.
Values may be sent and summed in bfloat16 or wider, within the bound.
A program may use at most 64 MiB of HBM per device.

v0:
```python
import jax
import jax.numpy as jnp
from jax import lax
from jax.sharding import PartitionSpec as P

E = 8192
eps_norm = 1e-05
eps_std = 0.0001


def gelu_slope(preactivation):
    value, pullback = jax.vjp(lambda t: jax.nn.gelu(t, approximate=True), preactivation)
    return pullback(jnp.ones_like(value))[0]


def shards(views, norm_scale_gain, norm_shift_bias, weight):
    n_batch = lax.axis_size("batch")
    n_col = lax.axis_size("col")
    local_rows = views.shape[1]
    sample_count = local_rows * n_batch
    scale = sample_count * E / 128.0
    hidden_float = views.astype(jnp.float32)
    total = lax.psum(jnp.sum(hidden_float, axis=1), "batch")
    batch_average = total[:, None, :] / sample_count
    centred = hidden_float - batch_average
    spread = lax.psum(jnp.sum(centred * centred, axis=1), "batch")
    var = spread[:, None, :] / sample_count
    inverse_deviation = 1.0 / jnp.sqrt(var + eps_norm)
    normalised_input = (hidden_float - batch_average) * inverse_deviation
    preactivation = norm_scale_gain * normalised_input + norm_shift_bias
    act = jax.nn.gelu(preactivation, approximate=True).astype(jnp.bfloat16)
    act_full = lax.all_gather(act, "col", axis=2, tiled=True)
    z_local = jnp.einsum(
        "vrk,kj->vrj", act_full, weight, preferred_element_type=jnp.float32
    ).astype(jnp.bfloat16)
    z_all = lax.all_gather(z_local, "batch", axis=1, tiled=True)
    zf_all = z_all.astype(jnp.float32)
    zmean = jnp.mean(zf_all, axis=1, keepdims=True)
    zc_all = zf_all - zmean
    zvar = jnp.sum(zc_all * zc_all, axis=1, keepdims=True) / (sample_count - 1)
    std = jnp.sqrt(zvar + eps_std)
    zcb_all = zc_all.astype(jnp.bfloat16)
    offset = lax.axis_index("batch") * local_rows
    zc_loc = lax.dynamic_slice_in_dim(zc_all, offset, local_rows, 1)
    zcb_loc = zc_loc.astype(jnp.bfloat16)
    diag = jnp.sum(jnp.square(zcb_all.astype(jnp.float32)), axis=1, keepdims=True)
    kernel_part = jnp.einsum("vrj,vmj->vrm", zcb_loc, zcb_all, preferred_element_type=jnp.float32)
    kernel = lax.psum(kernel_part, "col")
    kernel_b = kernel.astype(jnp.bfloat16)
    denom = float((sample_count - 1) ** 2 * E)
    coef = 4.0 * scale / denom
    hinge_coef = 25.0 * scale / (2.0 * E * (sample_count - 1))
    mask = jnp.where(std < 1.0, 1.0, 0.0)
    moved = jnp.einsum("vrm,vmj->vrj", kernel_b, zcb_all, preferred_element_type=jnp.float32)
    g_cov = coef * (moved - zcb_loc.astype(jnp.float32) * diag)
    g_var = -hinge_coef * mask * zc_loc / std
    summed = g_cov + g_var
    col_total = lax.psum(jnp.sum(summed, axis=1), "batch")
    zf_loc = z_local.astype(jnp.float32)
    diff = zf_loc[0] - zf_loc[1]
    g_inv = 50.0 * scale / (sample_count * E) * diff
    dz = summed - col_total[:, None, :] / sample_count + jnp.stack([g_inv, -g_inv])
    dzb = dz.astype(jnp.bfloat16)
    inv_share = jnp.sum(diff * diff) / (sample_count * E)
    hinge_share = jnp.sum(jnp.maximum(1.0 - std, 0.0)) / (2 * E)
    block_share = jnp.sum(kernel * kernel) / denom
    diag_share = jnp.sum(diag * diag) / denom
    share = 25.0 * inv_share + (25.0 * hinge_share - diag_share) / n_batch + block_share / n_col
    loss = lax.psum(share, ("batch", "col"))
    d_act_t = lax.psum_scatter(
        jnp.einsum("kj,vrj->kvr", weight, dzb, preferred_element_type=jnp.float32),
        "col",
        scatter_dimension=0,
        tiled=True,
    )
    d_act = jnp.transpose(d_act_t, (1, 2, 0))
    grad_weight = lax.psum_scatter(
        jnp.einsum("vrk,vrj->kj", act_full, dzb, preferred_element_type=jnp.float32),
        "batch",
        scatter_dimension=0,
        tiled=True,
    )
    preactivation_gradient = d_act * gelu_slope(preactivation)
    bias_gradient_sum, gain_gradient_sum = lax.psum(
        (
            jnp.sum(preactivation_gradient, axis=1),
            jnp.sum(preactivation_gradient * normalised_input, axis=1),
        ),
        "batch",
    )
    grad_bias = jnp.sum(bias_gradient_sum, axis=0)
    grad_gain = jnp.sum(gain_gradient_sum, axis=0)
    views_gradient = (
        norm_scale_gain
        * (
            preactivation_gradient
            - bias_gradient_sum[:, None, :] / sample_count
            - normalised_input * gain_gradient_sum[:, None, :] / sample_count
        )
        * inverse_deviation
    )
    return (loss, grad_weight, grad_gain, grad_bias, views_gradient)


def solution(mesh):
    placed = (P(None, "batch", "col"), P("col"), P("col"), P(None, "col"))
    return jax.shard_map(
        shards,
        mesh=mesh,
        in_specs=placed,
        out_specs=(P(), P("batch", "col"), P("col"), P("col"), P(None, "batch", "col")),
        check_vma=False,
    )
```

profile of v0, /device:TPU:1, one launch (start us, length us, event | category | flops | bytes accessed | tf_op | source)
XLA Modules:
  0.0 430.3 jit_solution(8545685748164966906)
XLA Ops:
  7.2 1.0 convert_reduce_fusion.1
  8.2 17.3 %psum.49 = f32[2,128]{1,0:T(2,128)S(1)} all-reduce(f32[2,128]{1,0:T(2,128)S(1)} %convert_reduce_fusion.1), channel_id=1, replica_groups=mesh['batch'=8,'col'=32] {'batch'}, use_global_device_ids=true, to_apply=%region_1.0 | all-reduce | flops 256 | bytes 2048 | tf_op jit(solution)/shard_map/psum | solution.py:23
  25.5 0.9 fusion.32
  26.4 10.8 %psum.50 = f32[2,128]{1,0:T(2,128)S(1)} all-reduce(f32[2,128]{1,0:T(2,128)S(1)} %fusion.32), channel_id=1, replica_groups=mesh['batch'=8,'col'=32] {'batch'}, use_global_device_ids=true, to_apply=%region_3.0 | all-reduce | flops 256 | bytes 2048 | tf_op jit(solution)/shard_map/psum | solution.py:26
  37.2 1.6 fusion.25
  38.8 0.0 all-gather.5.cloned.1.call-start
  38.8 56.4 %all-gather.3.cloned.1.call-done = bf16[2,128,4096]{2,1,0:T(8,128)(2,1)} async-done(((bf16[2,128,128]{2,1,0:T(8,128)(2,1)}), bf16[2,128,4096]{2,1,0:T(8,128)(2,1)}) %all-gather.3.cloned.1.call-update) | async-done | bytes 2097168 | tf_op jit(solution)/shard_map/all_gather | solution.py:32
  95.2 3.0 fusion.42
  98.2 32.8 %all-gather.5.cloned.1.call-done = bf16[2,1024,256]{2,1,0:T(8,128)(2,1)} async-done(((bf16[2,128,256]{2,1,0:T(8,128)(2,1)}), bf16[2,1024,256]{2,1,0:T(8,128)(2,1)}) %all-gather.5.cloned.1.call-update) | async-done | bytes 1048592 | tf_op jit(solution)/shard_map/all_gather | solution.py:36
  131.1 1.5 convert_reduce_fusion
  132.6 2.1 multiply_reduce_fusion
  134.7 1.3 copy-done.2
  136.0 1.5 fusion.10
  137.6 1.3 fusion.41
  138.8 1.3 fusion.37
  140.2 115.7 %all-reduce.3.cloned.1.call-done = f32[2,128,1024]{2,1,0:T(8,128)} async-done(((f32[2,128,1024]{2,1,0:T(8,128)}), f32[2,128,1024]{2,1,0:T(8,128)}) %all-reduce.3.cloned.1.call-update) | async-done | bytes 1048592 | tf_op jit(solution)/shard_map/psum | solution.py:48
  255.9 2.4 fusion.43
  258.3 13.7 %psum.53 = f32[2,256]{1,0:T(2,128)S(1)} all-reduce(f32[2,256]{1,0:T(2,128)S(1)} %get-tuple-element.23), channel_id=1, replica_groups=mesh['batch'=8,'col'=32] {'batch'}, use_global_device_ids=true, to_apply=%region_14.15 | all-reduce | flops 512 | bytes 4096 | tf_op jit(solution)/shard_map/psum | solution.py:58
  272.0 1.0 fusion.13
  272.9 2.7 convolution_bitcast_fusion
  275.7 0.0 reduce-scatter.3.cloned.1.call-start
  275.7 4.3 convolution_bitcast_fusion.1
  281.4 0.6 multiply_reduce_fusion.4
  282.7 0.9 multiply_reduce_fusion.2
  284.2 78.4 %psum.52 = f32[]{:T(128)} all-reduce(f32[]{:T(128)S(6)} %add.83), channel_id=1, replica_groups=mesh['batch'=8,'col'=32] {'batch','col'}, use_global_device_ids=true, to_apply=%region_12.13 | all-reduce | flops 1 | bytes 8 | tf_op jit(solution)/shard_map/psum | solution.py:69
  362.6 1.7 reduce-scatter.5.cloned.1.call-done
  364.4 1.0 fusion.39
  365.4 14.1 %all-reduce = (f32[2,128]{1,0:T(2,128)S(1)}, f32[2,128]{1,0:T(2,128)S(1)}) all-reduce(f32[2,128]{1,0:T(2,128)S(1)} %get-tuple-element.8, f32[2,128]{1,0:T(2,128)S(1)} %get-tuple-element.7), channel_id=1, replica_groups=mesh['batch'=8,'col'=32] {'batch'}, use_global_device_ids=true, to_apply=%region_18.19 | all-reduce | flops 512 | bytes 4096 | tf_op jit(solution)/shard_map/psum | solution.py:84
  379.5 0.5 reduce_sum.137
  380.1 0.5 broadcast_multiply_fusion.3
  380.6 0.7 fusion.31
  381.3 42.5 %reduce-scatter.3.cloned.1.call-done = f32[512,256]{1,0:T(8,128)} async-done(((f32[4096,256]{1,0:T(8,128)}), f32[512,256]{1,0:T(8,128)}) %reduce-scatter.3.cloned.1.call-update) | async-done | bytes 524304 | tf_op jit(solution)/shard_map/reduce_scatter | solution.py:77
  (27 shorter events, 0.3 us)
Async XLA Ops:
  7.2 88.0 %copy-start = (bf16[4096,256]{1,0:T(8,128)(2,1)S(1)}, bf16[4096,256]{1,0:T(8,128)(2,1)}, u32[]{:S(2)}) copy-start(bf16[4096,256]{1,0:T(8,128)(2,1)} %param.7) | copy-start | bytes 6291460
  7.2 88.0 %all-gather.3.cloned.1.call-start = ((), (), s32[]{:S(2)}) async-start(), calls=%async_computation.2 | async-start | bytes 2162688 | tf_op jit(solution)/shard_map/all_gather | solution.py:32
  38.8 92.3 %all-gather.5.cloned.1.call-start = ((), (), s32[]{:S(2)}) async-start(), calls=%async_computation.3 | async-start | bytes 1179648 | tf_op jit(solution)/shard_map/all_gather | solution.py:36
  98.2 157.7 %all-reduce.3.cloned.1.call-start = ((), (), s32[]{:S(2)}) async-start(), calls=%async_computation.4 | async-start | bytes 2097152 | tf_op jit(solution)/shard_map/psum | solution.py:48
  131.1 5.0 %copy-start.1 = (bf16[2,1024,256]{2,1,0:T(8,128)(2,1)S(1)}, bf16[2,1024,256]{2,1,0:T(8,128)(2,1)}, u32[]{:S(2)}) copy-start(bf16[2,1024,256]{2,1,0:T(8,128)(2,1)} %all-gather.5.cloned.1.call-done) | copy-start | bytes 3145732
  134.6 1.4 copy-start.2
  137.5 226.9 %reduce-scatter.5.cloned.1.call-start = ((), (), s32[]{:S(2)}) async-start(), calls=%async_computation.6 | async-start | bytes 4325376 | tf_op jit(solution)/shard_map/reduce_scatter | solution.py:70
  138.8 133.1 %copy-start.5 = (f32[1,128,256]{2,1,0:T(8,128)S(1)}, f32[1,128,256]{2,1,0:T(8,128)}, u32[]{:S(2)}) copy-start(f32[1,128,256]{2,1,0:T(8,128)} %get-tuple-element.13) | copy-start | bytes 393220
  275.7 148.1 %reduce-scatter.3.cloned.1.call-start = ((), (), s32[]{:S(2)}) async-start(), calls=%async_computation.5 | async-start | bytes 4718592 | tf_op jit(solution)/shard_map/reduce_scatter | solution.py:77
  280.0 2.7 copy-start.4
  280.0 84.3 %copy-start.3 = (bf16[2,128,128]{2,1,0:T(8,128)(2,1)S(1)}, bf16[2,128,128]{2,1,0:T(8,128)(2,1)}, u32[]{:S(2)}) copy-start(bf16[2,128,128]{2,1,0:T(8,128)(2,1)} %param.4) | copy-start | bytes 196612
  280.0 84.3 %copy-start.6 = (f32[128]{0:T(128)S(1)}, f32[128]{0:T(128)}, u32[]{:S(2)}) copy-start(f32[128]{0:T(128)} %param.5) | copy-start | bytes 1540
  280.0 84.3 %copy-start.7 = (f32[128]{0:T(128)S(1)}, f32[128]{0:T(128)}, u32[]{:S(2)}) copy-start(f32[128]{0:T(128)} %param.6) | copy-start | bytes 1540
Sparse Core Ops, SparseCore 0:
  38.9 56.2 all-gather.2
  98.3 32.7 all-gather.4
  137.6 118.2 all-reduce.2
  275.8 88.5 reduce-scatter.4
  367.3 56.3 reduce-scatter.2
where the time goes:
time: 431 us; the launch traced here: 430 us
  waiting for transfers between devices  249 us (58%)
  blocking collectives  134 us (31%)
  between operations  16.5 us (4%)
  other arithmetic  14.9 us (3%)
  matrix products  13.8 us (3%)
    psum x1, waiting for transfers between devices, shards(): kernel = lax.psum(kernel_part, 'col')  116 us
    psum x1, blocking collectives, shards(): loss = lax.psum(share, ('batch', 'col'))  78.4 us
    all_gather x1, waiting for transfers between devices, shards(): act_full = lax.all_gather(act, 'col', axis=2, tiled=True)  56.4 us
    reduce_scatter x1, waiting for transfers between devices, shards(): lax.psum_scatter(jnp.einsum('vrk,vrj->kj', act_full, dzb, preferred_eleme...  42.5 us
    all_gather x1, waiting for transfers between devices, shards(): z_all = lax.all_gather(z_local, 'batch', axis=1, tiled=True)  32.8 us
    psum x1, blocking collectives, shards(): total = lax.psum(jnp.sum(hidden_float, axis=1), 'batch')  17.3 us
    psum x1, blocking collectives, shards(): lax.psum((jnp.sum(preactivation_gradient, axis=1), jnp.sum(preactivation_...  14.1 us
    psum x1, blocking collectives, shards(): col_total = lax.psum(jnp.sum(summed, axis=1), 'batch')  13.7 us
  transfers between devices with their start and end apart: 5, of which 5 were waited for; matrix products, arithmetic and copies ran while one was open for 3% of the time, Pallas kernels for 0%

commit v1 on v0

--- a/solution.py
+++ b/solution.py
@@ -1,3 +1,4 @@
+import functools
 import jax
 import jax.numpy as jnp
 from jax import lax
@@ -6,6 +7,22 @@
 E = 8192
 eps_norm = 1e-05
 eps_std = 0.0001
+
+
+def shifts_all_read(w_in, axis_key):
+    t_next = jnp.concatenate(
+        lax.all_to_all(
+            jnp.stack([w_in for _ in range(lax.axis_size(axis_key))], axis=0),
+            axis_key,
+            split_axis=0,
+            concat_axis=0,
+        ),
+        axis=1,
+    )
+    return t_next
+
+
+vector_move = functools.partial(shifts_all_read, axis_key="batch")
 
 
 def gelu_slope(preactivation):
@@ -33,7 +50,7 @@
     z_local = jnp.einsum(
         "vrk,kj->vrj", act_full, weight, preferred_element_type=jnp.float32
     ).astype(jnp.bfloat16)
-    z_all = lax.all_gather(z_local, "batch", axis=1, tiled=True)
+    z_all = vector_move(z_local)
     zf_all = z_all.astype(jnp.float32)
     zmean = jnp.mean(zf_all, axis=1, keepdims=True)
     zc_all = zf_all - zmean

time: 431 us -> 421 us (0.977)
  waiting for transfers between devices: 249 us -> 238 us
  starting transfers between devices: 0.21 us -> 6.89 us
  other arithmetic: 14.9 us -> 10.5 us
    all_gather x1 -> x0, waiting for transfers between devices: 32.8 us -> none  [shards(): z_all = lax.all_gather(z_local, 'batch', axis=1, tiled=True)]
    all_to_all x0 -> x1, waiting for transfers between devices: none -> 29.2 us  [shifts_all_read(): lax.all_to_all(jnp.stack([w_in for _ in range(lax.axis_size(axis_key))],...]
    psum x1, waiting for transfers between devices: 116 us -> 107 us  [shards(): kernel = lax.psum(kernel_part, 'col')]
    all_to_all x0 -> x1, starting transfers between devices: none -> 6.73 us  [shifts_all_read(): lax.all_to_all(jnp.stack([w_in for _ in range(lax.axis_size(axis_key))],...]
where the time goes in v1:
time: 421 us
  waiting for transfers between devices  238 us (57%)
  blocking collectives  134 us (32%)
  between operations  16.6 us (4%)
  matrix products  13 us (3%)
  other arithmetic  10.5 us (2%)
  starting transfers between devices  6.89 us (2%)
    psum x1, waiting for transfers between devices, shards(): kernel = lax.psum(kernel_part, 'col')  107 us
    psum x1, blocking collectives, shards(): loss = lax.psum(share, ('batch', 'col'))  78.4 us
    all_gather x1, waiting for transfers between devices, shards(): act_full = lax.all_gather(act, 'col', axis=2, tiled=True)  56.4 us
    reduce_scatter x1, waiting for transfers between devices, shards(): lax.psum_scatter(jnp.einsum('vrk,vrj->kj', act_full, dzb, preferred_eleme...  42.9 us
    all_to_all x1, waiting for transfers between devices, shifts_all_read(): lax.all_to_all(jnp.stack([w_in for _ in range(lax.axis_size(axis_key))],...  29.2 us
    psum x1, blocking collectives, shards(): total = lax.psum(jnp.sum(hidden_float, axis=1), 'batch')  17.3 us
    psum x1, blocking collectives, shards(): col_total = lax.psum(jnp.sum(summed, axis=1), 'batch')  13.7 us
    psum x1, blocking collectives, shards(): lax.psum((jnp.sum(preactivation_gradient, axis=1), jnp.sum(preactivation_...  13.4 us
  transfers between devices with their start and end apart: 5, of which 5 were waited for; matrix products, arithmetic and copies ran while one was open for 3% of the time, Pallas kernels for 0%

profile of v1, /device:TPU:1, one launch (start us, length us, event | category | flops | bytes accessed | tf_op | source)
XLA Modules:
  0.0 420.7 jit_solution(186589146779951502)
XLA Ops:
  7.2 1.0 convert_reduce_fusion
  8.2 17.3 %psum.49 = f32[2,128]{1,0:T(2,128)S(1)} all-reduce(f32[2,128]{1,0:T(2,128)S(1)} %convert_reduce_fusion), channel_id=1, replica_groups=mesh['batch'=8,'col'=32] {'batch'}, use_global_device_ids=true, to_apply=%region_1.0 | all-reduce | flops 256 | bytes 2048 | tf_op jit(solution)/shard_map/psum | solution.py:40
  25.5 0.9 fusion.32
  26.4 10.8 %psum.50 = f32[2,128]{1,0:T(2,128)S(1)} all-reduce(f32[2,128]{1,0:T(2,128)S(1)} %fusion.32), channel_id=1, replica_groups=mesh['batch'=8,'col'=32] {'batch'}, use_global_device_ids=true, to_apply=%region_3.0 | all-reduce | flops 256 | bytes 2048 | tf_op jit(solution)/shard_map/psum | solution.py:43
  37.2 1.6 fusion.25
  38.8 56.4 %all-gather.2.cloned.1.call-done = bf16[2,128,4096]{2,1,0:T(8,128)(2,1)} async-done(((bf16[2,128,128]{2,1,0:T(8,128)(2,1)}), bf16[2,128,4096]{2,1,0:T(8,128)(2,1)}) %all-gather.2.cloned.1.call-update) | async-done | bytes 2097168 | tf_op jit(solution)/shard_map/all_gather | solution.py:49
  95.2 2.3 fusion.42
  97.5 1.1 stack.4
  98.6 6.7 %all-to-all-start = ((bf16[8,2,128,256]{3,2,1,0:T(8,128)(2,1)}), bf16[8,2,128,256]{3,2,1,0:T(8,128)(2,1)S(1)}, u32[]{:S(2)}, u32[]{:S(2)}) async-start(bf16[8,2,128,256]{3,2,1,0:T(8,128)(2,1)} %stack.4), calls=%async_computation | async-start | bytes 2097152 | tf_op jit(solution)/shard_map/all_to_all | solution.py:14
  105.4 29.2 %all-to-all-done = bf16[8,2,128,256]{3,2,1,0:T(8,128)(2,1)S(1)} async-done(((bf16[8,2,128,256]{3,2,1,0:T(8,128)(2,1)}), bf16[8,2,128,256]{3,2,1,0:T(8,128)(2,1)S(1)}, u32[]{:S(2)}, u32[]{:S(2)}) %all-to-all-start) | async-done | bytes 1048608 | tf_op jit(solution)/shard_map/all_to_all | solution.py:14
  134.6 0.2 fusion.3
  134.8 0.2 convert_bitcast_fusion
  135.3 1.3 copy-done.1
  136.7 1.5 fusion.11
  138.2 1.3 fusion.41
  139.5 0.3 multiply_reduce_fusion
  139.8 0.6 fusion.37
  140.4 107.0 %all-reduce.3.cloned.1.call-done = f32[2,128,1024]{2,1,0:T(8,128)} async-done(((f32[2,128,1024]{2,1,0:T(8,128)}), f32[2,128,1024]{2,1,0:T(8,128)}) %all-reduce.3.cloned.1.call-update) | async-done | bytes 1048592 | tf_op jit(solution)/shard_map/psum | solution.py:65
  247.4 2.2 fusion.43
  249.6 13.7 %psum.53 = f32[2,256]{1,0:T(2,128)S(1)} all-reduce(f32[2,256]{1,0:T(2,128)S(1)} %get-tuple-element.22), channel_id=1, replica_groups=mesh['batch'=8,'col'=32] {'batch'}, use_global_device_ids=true, to_apply=%region_14.15 | all-reduce | flops 512 | bytes 4096 | tf_op jit(solution)/shard_map/psum | solution.py:75
  263.4 2.7 convolution_bitcast_fusion
  266.2 4.3 %convolution_bitcast_fusion.1 = f32[4096,256]{1,0:T(8,128)} fusion(bf16[2,128,4096]{2,1,0:T(8,128)(2,1)} %all-gather.2.cloned.1.call-done, bf16[2,128,256]{2,1,0:T(8,128)(2,1)S(1)} %fusion.13), kind=kOutput, calls=%fused_computation.1 | convolution fusion | flops 536870912 | bytes 6422528 | tf_op jit(solution)/shard_map/vrk,vrj->kj/dot_general | solution.py:95
  271.9 0.6 multiply_reduce_fusion.4
  273.1 0.9 multiply_reduce_fusion.2
  274.7 78.4 %psum.52 = f32[]{:T(128)} all-reduce(f32[]{:T(128)S(6)} %add.83), channel_id=1, replica_groups=mesh['batch'=8,'col'=32] {'batch','col'}, use_global_device_ids=true, to_apply=%region_12.13 | all-reduce | flops 1 | bytes 8 | tf_op jit(solution)/shard_map/psum | solution.py:86
  353.1 2.0 reduce-scatter.5.cloned.1.call-done
  355.1 1.0 fusion.39
  356.1 13.4 %all-reduce = (f32[2,128]{1,0:T(2,128)S(1)}, f32[2,128]{1,0:T(2,128)S(1)}) all-reduce(f32[2,128]{1,0:T(2,128)S(1)} %get-tuple-element.8, f32[2,128]{1,0:T(2,128)S(1)} %get-tuple-element.7), channel_id=1, replica_groups=mesh['batch'=8,'col'=32] {'batch'}, use_global_device_ids=true, to_apply=%region_18.19 | all-reduce | flops 512 | bytes 4096 | tf_op jit(solution)/shard_map/psum | solution.py:101
  369.5 0.5 reduce_sum.137
  370.1 0.5 broadcast_multiply_fusion.3
  370.6 0.7 fusion.31
  371.3 42.9 %reduce-scatter.3.cloned.1.call-done = f32[512,256]{1,0:T(8,128)} async-done(((f32[4096,256]{1,0:T(8,128)}), f32[512,256]{1,0:T(8,128)}) %reduce-scatter.3.cloned.1.call-update) | async-done | bytes 524304 | tf_op jit(solution)/shard_map/reduce_scatter | solution.py:94
  (28 shorter events, 0.6 us)
Async XLA Ops:
  7.2 88.0 %copy-start = (bf16[4096,256]{1,0:T(8,128)(2,1)S(1)}, bf16[4096,256]{1,0:T(8,128)(2,1)}, u32[]{:S(2)}) copy-start(bf16[4096,256]{1,0:T(8,128)(2,1)} %param.7) | copy-start | bytes 6291460
  7.2 88.0 %all-gather.2.cloned.1.call-start = ((), (), s32[]{:S(2)}) async-start(), calls=%async_computation.3 | async-start | bytes 2162688 | tf_op jit(solution)/shard_map/all_gather | solution.py:49
  98.6 36.0 %all-to-all-start = ((bf16[8,2,128,256]{3,2,1,0:T(8,128)(2,1)}), bf16[8,2,128,256]{3,2,1,0:T(8,128)(2,1)S(1)}, u32[]{:S(2)}, u32[]{:S(2)}) async-start(bf16[8,2,128,256]{3,2,1,0:T(8,128)(2,1)} %stack.4), calls=%async_computation | async-start | bytes 2097152 | tf_op jit(solution)/shard_map/all_to_all | solution.py:14
  105.3 142.0 %all-reduce.3.cloned.1.call-start = ((), (), s32[]{:S(2)}) async-start(), calls=%async_computation.4 | async-start | bytes 2097152 | tf_op jit(solution)/shard_map/psum | solution.py:65
  135.3 1.4 copy-start.1
  138.2 216.9 %reduce-scatter.5.cloned.1.call-start = ((), (), s32[]{:S(2)}) async-start(), calls=%async_computation.6 | async-start | bytes 4325376 | tf_op jit(solution)/shard_map/reduce_scatter | solution.py:87
  139.5 123.8 %copy-start.4 = (f32[1,128,256]{2,1,0:T(8,128)S(1)}, f32[1,128,256]{2,1,0:T(8,128)}, u32[]{:S(2)}) copy-start(f32[1,128,256]{2,1,0:T(8,128)} %get-tuple-element.13) | copy-start | bytes 393220
  266.1 148.1 %reduce-scatter.3.cloned.1.call-start = ((), (), s32[]{:S(2)}) async-start(), calls=%async_computation.5 | async-start | bytes 4718592 | tf_op jit(solution)/shard_map/reduce_scatter | solution.py:94
  270.4 2.7 copy-start.2
  270.5 84.6 %copy-start.3 = (bf16[2,128,128]{2,1,0:T(8,128)(2,1)S(1)}, bf16[2,128,128]{2,1,0:T(8,128)(2,1)}, u32[]{:S(2)}) copy-start(bf16[2,128,128]{2,1,0:T(8,128)(2,1)} %param.4) | copy-start | bytes 196612
  270.5 84.6 %copy-start.5 = (f32[128]{0:T(128)S(1)}, f32[128]{0:T(128)}, u32[]{:S(2)}) copy-start(f32[128]{0:T(128)} %param.5) | copy-start | bytes 1540
  270.5 84.6 %copy-start.6 = (f32[128]{0:T(128)S(1)}, f32[128]{0:T(128)}, u32[]{:S(2)}) copy-start(f32[128]{0:T(128)} %param.6) | copy-start | bytes 1540
Sparse Core Ops, SparseCore 0:
  38.9 56.2 all-gather.1
  138.3 109.0 all-reduce.2
  266.2 88.7 reduce-scatter.4
  358.0 56.1 reduce-scatter.2
